TPU v7x, 32 devices: a whole 2x2x4 slice. The times are simulated.
32 devices in a mesh: tm: 8 (over z, x), state: 4 (over y, core).
Axes of the slice: x: 2, y: 2, z: 4, core: 2. Of those that a mesh axis runs over, the one named last changes fastest.
Arguments:
- dyn_cols: int32 [256, 8, 3], P('tm', 'state'), may hold values from 0 to 7, as said below
- dyn_vals: bfloat16 [256, 8, 64, 192], P('tm', 'state'), may hold values from -1 to 1
- obs_blocks: int32 [256, 2], P('tm'), may hold values from 0 to 7
- obs_op: bfloat16 [256, 64, 128], P('tm'), may hold values from -0.75 to 0.75
- obs_counts: int32 [256], P('tm'), may hold values from 32 to 128, as said below
- obs_values: float32 [256, 128], P('tm'), may hold values from -6 to 6
- gain: bfloat16 [256, 512, 128], P('tm', 'state'), may hold values from -0.0078125 to 0.0078125
- sources: float32 [256, 512], P('tm', 'state'), may hold values from -0.625 to 0.625
- prior: float32 [512], replicated, may hold values from -6 to 6
Outputs:
- filtered: float32 [256, 512], P('tm', 'state')
Inputs may be any that keep to these rules, and one draw needn't show every extreme that they name: `dyn_cols`: for every step and block row i, the first entry is i itself and the 3 entries are distinct block columns. `obs_counts`: some step has all 128 observations present.
All inputs are finite; a program needn't handle non-finite values.
Results may differ from a plain program's by a relative error of at most 0.0003.
The roundings to bfloat16 on the way count: a program that leaves them out, or rounds other values in their place, can miss the bound.
Values may be sent and summed in bfloat16 or wider, within the bound.
No kernel may reach another device: no remote copies, remote signals or barrier semaphores. Data moves between devices by JAX's collectives and lax.ppermute only.
A program may use at most 128 MiB of HBM per device.

v0:
```python
import jax
import jax.numpy as jnp
from jax import lax
from jax.sharding import PartitionSpec as P

NS = 512
BS = 64
KF = 3
OBS = 128
NB = 8
OB = 2
HIGHEST = lax.Precision.HIGHEST


def shifted(shard, axis, by):
    devices = lax.axis_size(axis)
    pairs = [(i, i + by) for i in range(devices) if 0 <= i + by < devices]
    return lax.ppermute(shard, axis, pairs)


def split_product(matrix, operand):
    leading = operand.astype(jnp.bfloat16)
    remainder = (operand - lax.optimization_barrier(leading).astype(jnp.float32)).astype(
        jnp.bfloat16
    )
    return jnp.dot(matrix, leading, preferred_element_type=jnp.float32) + jnp.dot(
        matrix, remainder, preferred_element_type=jnp.float32
    )


def body(dyn_cols, dyn_vals, obs_blocks, obs_op, obs_counts, obs_values, gain, sources, prior):
    step_count = dyn_vals.shape[0]
    local_blocks = dyn_vals.shape[1]
    local_rows = local_blocks * BS
    state_index = lax.axis_index("state")
    time_index = lax.axis_index("tm")
    onehot = (dyn_cols[..., None] == jnp.arange(NB)).astype(jnp.bfloat16)
    blocks = dyn_vals.reshape(step_count, local_blocks, BS, KF, BS)
    forward = jnp.einsum("tikc,tiakb->tiacb", onehot, blocks, preferred_element_type=jnp.float32)
    forward = forward.reshape(step_count, local_blocks, BS, NS)
    forward_narrow = forward.astype(jnp.bfloat16)
    owned = state_index * local_blocks + jnp.arange(local_blocks)
    select = obs_blocks[:, :, None] == owned[None, None, :]
    selected = jnp.einsum(
        "tos,tsbn->tobn",
        select.astype(jnp.bfloat16),
        forward_narrow,
        preferred_element_type=jnp.float32,
    ).astype(jnp.bfloat16)
    operator_blocks = obs_op.reshape(step_count, BS, OB, BS)
    image_part = jnp.einsum(
        "tboa,tobn->toan", operator_blocks, selected, preferred_element_type=jnp.float32
    )
    image_part = image_part.reshape(step_count, OBS, NS)
    source_sel = jnp.einsum(
        "tos,tsb->tob",
        select.astype(jnp.float32),
        sources.reshape(step_count, local_blocks, BS),
        precision=HIGHEST,
    )
    source_part = jnp.einsum(
        "tboa,tob->toa", operator_blocks.astype(jnp.float32), source_sel, precision=HIGHEST
    )
    source_part = source_part.reshape(step_count, OBS)
    image_sum, source_sum = (
        lax.psum(image_part.astype(jnp.bfloat16), "state").astype(jnp.float32),
        lax.psum(source_part.astype(jnp.bfloat16), "state").astype(jnp.float32),
    )
    active = jnp.arange(OBS)[None, :] < obs_counts[:, None]
    masked = jnp.where(
        active[:, :, None], image_sum.astype(jnp.bfloat16), jnp.zeros((), jnp.bfloat16)
    )
    source_image = lax.optimization_barrier(source_sum.astype(jnp.bfloat16)).astype(jnp.float32)
    innovation = jnp.where(active, obs_values - source_image, 0.0)
    correction = jnp.einsum("tro,ton->trn", gain, masked, preferred_element_type=jnp.float32)
    element = (forward.reshape(step_count, local_rows, NS) - correction).astype(jnp.bfloat16)
    offset = sources + jnp.einsum(
        "tro,to->tr", gain.astype(jnp.float32), innovation, precision=HIGHEST
    )
    full_elements = lax.all_gather(element, "state", axis=1, tiled=True)
    full_offsets = lax.all_gather(offset, "state", axis=1, tiled=True)
    start_cols = (
        jnp.arange(NS)[:, None] == (state_index * local_rows + jnp.arange(local_rows))[None, :]
    ).astype(jnp.float32)

    def compose(carry, inputs):
        product, vector = carry
        matrix, shift_term = inputs
        product = split_product(matrix, product)
        vector = split_product(matrix, vector) + shift_term
        return ((product, vector), None)

    (column_product, span_offset), _ = lax.scan(
        compose, (start_cols, jnp.zeros((NS,), jnp.float32)), (full_elements, full_offsets)
    )
    span_matrix = lax.all_gather(column_product, "state", axis=1, tiled=True)
    first_span = time_index == 0

    def hand_over(turn, current):
        leaving = jnp.dot(span_matrix, current, precision=HIGHEST) + span_offset
        arriving = shifted(leaving, "tm", 1)
        return jnp.where(first_span, prior, arriving)

    entry = lax.fori_loop(0, lax.axis_size("tm") - 1, hand_over, prior)

    def sweep(current, inputs):
        matrix, shift_term = inputs
        new_mean = split_product(matrix, current) + shift_term
        return (new_mean, lax.dynamic_slice_in_dim(new_mean, state_index * local_rows, local_rows))

    _, filtered = lax.scan(sweep, entry, (full_elements, full_offsets))
    return filtered


def solution(mesh):
    return jax.shard_map(
        body,
        mesh=mesh,
        in_specs=(
            P("tm", "state", None),
            P("tm", "state", None, None),
            P("tm", None),
            P("tm", None, None),
            P("tm"),
            P("tm", None),
            P("tm", "state", None),
            P("tm", "state"),
            P(),
        ),
        out_specs=P("tm", "state"),
        check_vma=False,
    )
```

profile of v0, /device:TPU:8, one launch (start us, length us, event | category | flops | bytes accessed | tf_op | source)
XLA Modules:
  0.0 674.5 jit_solution(3673502673892375149)
XLA Ops:
  10.6 4.5 copy.18
  15.1 7.1 %copy.19 = bf16[32,2,64,3,64]{4,3,2,1,0:T(4,128)(2,1)} copy(bf16[32,2,64,3,64]{2,4,3,1,0:T(8,128)(2,1)} %bitcast.140) | data formatting | bytes 3145728 | tf_op jit(solution)/shard_map/reshape | solution.py:38
  22.3 10.6 %fusion.48 = (bf16[32,2,64,8,64]{4,3,2,1,0:T(8,128)(2,1)}, f32[32,2,64,8,64]{4,3,2,1,0:T(8,128)}) fusion(bf16[32,2,64,3,64]{4,3,2,1,0:T(4,128)(2,1)} %copy.19, s32[32,2,3]{2,1,0:T(2,128)S(1)} %copy.17), kind=kOutput, calls=%fused_computation.66 | convolution fusion | flops 14681600 | bytes 14156544 | tf_op jit(solution)/shard_map/tikc,tiakb->tiacb/dot_general | solution.py:39
  32.9 11.8 %convert_element_type.77 = bf16[32,2,64,512]{3,2,1,0:T(8,128)(2,1)} reshape(bf16[32,2,64,8,64]{4,3,2,1,0:T(8,128)(2,1)} %get-tuple-element.218) | data formatting | bytes 8388608 | tf_op jit(solution)/shard_map/convert_element_type | solution.py:41
  44.7 8.7 %fusion.28 = bf16[32,2,64,512]{3,1,2,0:T(2,128)(2,1)S(1)} fusion(bf16[32,2,64,512]{3,2,1,0:T(8,128)(2,1)} %convert_element_type.77, s32[2]{0:T(128)S(1)} %iota_add_fusion, s32[32,2]{1,0:T(8,128)S(1)} %copy.20), kind=kOutput, calls=%fused_computation.42 | convolution fusion | flops 8388736 | bytes 8388872 | tf_op jit(solution)/shard_map/tos,tsbn->tobn/dot_general | solution.py:44
  56.7 6.5 copy.22
  63.2 14.5 %reshape_reshape.3 = f32[32,128,512]{2,1,0:T(8,128)} reshape(f32[32,2,64,8,64]{4,3,2,1,0:T(8,128)} %get-tuple-element.219) | data formatting | bytes 16777216 | tf_op jit(solution)/shard_map/reshape;reshape | solution.py:76
  77.7 9.0 %copy.23 = f32[32,128,512]{1,2,0:T(8,128)} copy(f32[32,128,512]{2,1,0:T(8,128)} %reshape_reshape.3) | data formatting | bytes 16777216 | tf_op jit(solution)/shard_map/reshape;reshape | solution.py:76
  86.8 63.2 %all-reduce.2.cloned.1.call-done = bf16[32,128,512]{1,2,0:T(8,128)(2,1)} async-done(((bf16[32,128,512]{1,2,0:T(8,128)(2,1)}), bf16[32,128,512]{1,2,0:T(8,128)(2,1)}) %all-reduce.2.cloned.1.call-update) | async-done | bytes 4194320 | tf_op jit(solution)/shard_map/psum | solution.py:66
  150.0 7.9 %fusion.23 = bf16[32,128,512]{1,2,0:T(8,128)(2,1)} fusion(f32[32,128,512]{1,2,0:T(8,128)} %copy.23, bf16[32,128,128]{2,1,0:T(8,128)(2,1)S(1)} %copy-done, bf16[32,128,512]{1,2,0:T(8,128)(2,1)} %all-reduce.2.cloned.1.call-done, pred[32,128]{1,0:T(8,128)(4,1)S(1)} %iota_compare_fusion.2), kind=kOutput, calls=%fused_computation.36 | convolution fusion | flops 543162368 | bytes 17829888 | tf_op jit(solution)/shard_map/tro,ton->trn/dot_general | solution.py:75
  160.0 6.4 psum.15
  168.3 5.5 all_gather.10
  173.8 92.7 %all-gather.3.cloned.1.call-done = bf16[32,512,512]{1,2,0:T(8,128)(2,1)} async-done(((bf16[32,128,512]{1,2,0:T(8,128)(2,1)}), bf16[32,512,512]{1,2,0:T(8,128)(2,1)}) %all-gather.3.cloned.1.call-update) | async-done | bytes 16777232 | tf_op jit(solution)/shard_map/all_gather | solution.py:80
  266.5 22.5 %copy.24 = bf16[32,512,512]{2,1,0:T(8,128)(2,1)} copy(bf16[32,512,512]{1,2,0:T(8,128)(2,1)} %all-gather.3.cloned.1.call-done) | data formatting | bytes 33554432
  289.1 173.2 %while.42 = (s32[]{:T(128)}, f32[512,128]{1,0:T(8,128)S(1)}, f32[512]{0:T(512)S(1)}, bf16[32,512,512]{2,1,0:T(8,128)(2,1)}, f32[32,512]{1,0:T(8,128)S(1)}) while((s32[]{:T(128)}, f32[512,128]{1,0:T(8,128)S(1)}, f32[512]{0:T(512)S(1)}, bf16[32,512,512]{2,1,0:T(8,128)(2,1)}, f32[32,512]{1,0:T(8,128)S(1)}) %tuple.69), condition=%wide.region_3.4_spmd.clone.clone, body=%wide.region_2.3_spmd.clone.sunk.clone | while | flops 135597568 | bytes 4355172 | solution.py:93
  463.1 16.9 %all-gather.5.cloned.1.call-done = f32[512,512]{1,0:T(8,128)} async-done(((f32[512,128]{1,0:T(8,128)}), f32[512,512]{1,0:T(8,128)}) %all-gather.5.cloned.1.call-update) | async-done | bytes 1048592 | tf_op jit(solution)/shard_map/all_gather | solution.py:96
  480.0 60.1 %while.40 = (s32[]{:T(128)}, f32[512]{0:T(512)S(1)}, pred[]{:T(512)}, f32[512,512]{1,0:T(8,128)}, f32[512]{0:T(512)S(1)}, /*index=5*/f32[512]{0:T(512)S(1)}) while((s32[]{:T(128)}, f32[512]{0:T(512)S(1)}, pred[]{:T(512)}, f32[512,512]{1,0:T(8,128)}, f32[512]{0:T(512)S(1)}, /*index=5*/f32[512]{0:T(512)S(1)}) %tuple.86), condition=%wide.region_5.6_spmd.clone, body=%wide.region_4.5_spmd.sunk.clone | while | flops 3146754 | bytes 1073262 | solution.py:104
  493.3 3.9 collective-permute-done
  501.3 4.4 collective-permute-done
  509.9 4.4 collective-permute-done
  518.5 4.4 collective-permute-done
  527.1 4.4 collective-permute-done
  535.7 4.4 collective-permute-done
  540.2 127.8 %while.41 = (s32[]{:T(128)}, f32[512]{0:T(512)S(1)}, f32[32,128]{1,0:T(8,128)}, bf16[32,512,512]{2,1,0:T(8,128)(2,1)}, f32[32,512]{1,0:T(8,128)S(1)}, /*index=5*/s32[]{:T(128)}) while((s32[]{:T(128)}, f32[512]{0:T(512)S(1)}, f32[32,128]{1,0:T(8,128)}, bf16[32,512,512]{2,1,0:T(8,128)(2,1)}, f32[32,512]{1,0:T(8,128)S(1)}, ...), condition=%wide.region_7.8_spmd.clone, body=%wide.region_6.7_spmd.sunk.clone | while | flops 1051650 | bytes 1080417 | solution.py:111
  (770 shorter events, 344.4 us)
Async XLA Ops:
  6.5 143.4 %copy-start = (bf16[32,128,128]{2,1,0:T(8,128)(2,1)S(1)}, bf16[32,128,128]{2,1,0:T(8,128)(2,1)}, u32[]{:S(2)}) copy-start(bf16[32,128,128]{2,1,0:T(8,128)(2,1)} %param.21) | copy-start | bytes 3145732
  6.5 143.4 %all-reduce.2.cloned.1.call-start = ((), (), s32[]{:S(2)}) async-start(), calls=%async_computation | async-start | bytes 8388608 | tf_op jit(solution)/shard_map/psum | solution.py:66
  63.2 203.3 %all-gather.3.cloned.1.call-start = ((), (), s32[]{:S(2)}) async-start(), calls=%async_computation.1 | async-start | bytes 20971520 | tf_op jit(solution)/shard_map/all_gather | solution.py:80
  77.7 9.0 %copy-start.5 = (s32[32]{0:T(128)S(1)}, s32[32]{0:T(128)}, u32[]{:S(2)}) copy-start(s32[32]{0:T(128)} %param.19) | copy-start | bytes 388
  157.9 0.7 copy-start.3
  157.9 8.6 %copy-start.4 = (f32[32,128]{1,0:T(8,128)S(1)}, f32[32,128]{1,0:T(8,128)}, u32[]{:S(2)}) copy-start(f32[32,128]{1,0:T(8,128)} %param.20) | copy-start | bytes 49156
  157.9 322.1 %all-gather.5.cloned.1.call-start = ((), (), s32[]{:S(2)}) async-start(), calls=%async_computation.2 | async-start | bytes 1310720 | tf_op jit(solution)/shard_map/all_gather | solution.py:96
  289.1 174.0 %copy-start.2 = (f32[512]{0:T(512)S(1)}, f32[512]{0:T(512)}, u32[]{:S(2)}) copy-start(f32[512]{0:T(512)} %param.23) | copy-start | bytes 6148
  462.3 0.7 copy-start.1
  482.2 6.4 collective-permute-start
  490.8 6.4 collective-permute-start
  499.4 6.4 collective-permute-start
  508.0 6.4 collective-permute-start
  516.6 6.4 collective-permute-start
  525.2 6.4 collective-permute-start
  533.8 6.4 collective-permute-start
Sparse Core Ops, SparseCore 0:
  63.3 86.6 all-reduce.1
  158.0 108.4 all-gather.2
  463.2 16.8 all-gather.4
where the time goes:
time: 687 us; the launch traced here: 674 us
  matrix products  299 us (44%)
  waiting for transfers between devices  202 us (29%)
  local copies, waits for them, and re-layouts  127 us (18%)
  starting transfers between devices  15.6 us (2%)
  between operations  13.2 us (2%)
  blocking collectives  11.9 us (2%)
    dot_general x96, matrix products, split_product(): jnp.dot(matrix, leading, preferred_element_type=jnp.float32)  126 us
    dot_general x96, matrix products, split_product(): jnp.dot(matrix, remainder, preferred_element_type=jnp.float32)  125 us
    all_gather x1, waiting for transfers between devices, body(): full_elements = lax.all_gather(element, 'state', axis=1, tiled=True)  92.7 us
    psum x1, waiting for transfers between devices, body(): lax.psum(image_part.astype(jnp.bfloat16), 'state').astype(jnp.float32)  63.2 us
    dynamic_update_slice x32, local copies, waits for them, and re-layouts, body(): _, filtered = lax.scan(sweep, entry, (full_elements, full_offsets))  41.3 us
    unnamed x17, local copies, waits for them, and re-layouts  30 us
    ppermute x7, waiting for transfers between devices, shifted(): return lax.ppermute(shard, axis, pairs)  29.1 us
    another operation x2, local copies, waits for them, and re-layouts, body(): forward.reshape(step_count, local_rows, NS) - correction  23.5 us
  transfers between devices with their start and end apart: 10, of which 10 were waited for; matrix products, arithmetic and copies ran while one was open for 4% of the time, Pallas kernels for 0%

commit v1 on v0

--- a/solution.py
+++ b/solution.py
@@ -10,6 +10,22 @@
 NB = 8
 OB = 2
 HIGHEST = lax.Precision.HIGHEST
+
+
+def collect(x, axis, dim):
+    ways, here, step = (lax.axis_size(axis), lax.axis_index(axis), x.shape[dim])
+    shape = [n * ways if d == dim else n for d, n in enumerate(x.shape)]
+    full = lax.dynamic_update_slice_in_dim(jnp.zeros(shape, x.dtype), x, here * step, axis=dim)
+    going_up = going_down = x
+    for far in range(1, ways // 2 + 1):
+        going_up = lax.ppermute(going_up, axis, [(d, (d + 1) % ways) for d in range(ways)])
+        full = lax.dynamic_update_slice_in_dim(full, going_up, (here - far) % ways * step, axis=dim)
+        if 2 * far < ways:
+            going_down = lax.ppermute(going_down, axis, [(d, (d - 1) % ways) for d in range(ways)])
+            full = lax.dynamic_update_slice_in_dim(
+                full, going_down, (here + far) % ways * step, axis=dim
+            )
+    return full
 
 
 def shifted(shard, axis, by):
@@ -77,7 +93,7 @@
     offset = sources + jnp.einsum(
         "tro,to->tr", gain.astype(jnp.float32), innovation, precision=HIGHEST
     )
-    full_elements = lax.all_gather(element, "state", axis=1, tiled=True)
+    full_elements = collect(element, "state", 1)
     full_offsets = lax.all_gather(offset, "state", axis=1, tiled=True)
     start_cols = (
         jnp.arange(NS)[:, None] == (state_index * local_rows + jnp.arange(local_rows))[None, :]

time: 687 us -> 748 us (1.089)
  blocking collectives: 11.9 us -> 53.2 us
  local copies, waits for them, and re-layouts: 127 us -> 147 us
    all_gather x1 -> x0, waiting for transfers between devices: 92.7 us -> none  [body(): full_elements = lax.all_gather(element, 'state', axis=1, tiled=True)]
    ppermute x0 -> x3, waiting for transfers between devices: none -> 90.4 us  [the longest x2 90.4 us: collect(): lax.ppermute(going_up, axis, [(d, (d + 1) % ways) for d in range(ways)])]
    psum x1, blocking collectives: 6.43 us -> 47.8 us  [body(): lax.psum(source_part.astype(jnp.bfloat16), 'state').astype(jnp.float32)]
    unnamed x17 -> x26, local copies, waits for them, and re-layouts: 30 us -> 5.51 us
    ppermute x0 -> x3, local copies, waits for them, and re-layouts: none -> 19.5 us  [the longest x2 13 us: collect(): lax.ppermute(going_up, axis, [(d, (d + 1) % ways) for d in range(ways)])]
    dynamic_update_slice x0 -> x4, local copies, waits for them, and re-layouts: none -> 14 us  [the longest x2 9.26 us: collect(): lax.dynamic_update_slice_in_dim(full, going_up, (here - far) % ways * ste...]
  transfers between devices with their start and end apart: 10 -> 12, of which waited for: 10 -> 10; matrix products, arithmetic and copies ran while one was open for 4% -> 8% of each run, Pallas kernels for 0% -> 0%
where the time goes in v1:
time: 748 us; the launch traced here: 736 us
  matrix products  299 us (40%)
  waiting for transfers between devices  200 us (27%)
  local copies, waits for them, and re-layouts  147 us (20%)
  blocking collectives  53.2 us (7%)
  starting transfers between devices  17.3 us (2%)
  between operations  13.5 us (2%)
    dot_general x96, matrix products, split_product(): jnp.dot(matrix, leading, preferred_element_type=jnp.float32)  126 us
    dot_general x96, matrix products, split_product(): jnp.dot(matrix, remainder, preferred_element_type=jnp.float32)  125 us
    ppermute x2, waiting for transfers between devices, collect(): lax.ppermute(going_up, axis, [(d, (d + 1) % ways) for d in range(ways)])  90.4 us
    psum x1, waiting for transfers between devices, body(): lax.psum(image_part.astype(jnp.bfloat16), 'state').astype(jnp.float32)  63.2 us
    psum x1, blocking collectives, body(): lax.psum(source_part.astype(jnp.bfloat16), 'state').astype(jnp.float32)  47.8 us
    dynamic_update_slice x32, local copies, waits for them, and re-layouts, body(): _, filtered = lax.scan(sweep, entry, (full_elements, full_offsets))  41.3 us
    ppermute x7, waiting for transfers between devices, shifted(): return lax.ppermute(shard, axis, pairs)  29.1 us
    another operation x2, local copies, waits for them, and re-layouts, body(): forward.reshape(step_count, local_rows, NS) - correction  23.5 us
  transfers between devices with their start and end apart: 12, of which 10 were waited for; matrix products, arithmetic and copies ran while one was open for 8% of the time, Pallas kernels for 0%

profile of v1, /device:TPU:8, one launch (start us, length us, event | category | flops | bytes accessed | tf_op | source)
XLA Modules:
  0.0 735.7 jit_solution(11698746974586181651)
XLA Ops:
  6.5 4.6 copy.20
  11.1 7.2 copy.21
  18.4 10.6 %fusion.48 = (bf16[32,2,64,8,64]{4,3,2,1,0:T(8,128)(2,1)}, f32[32,2,64,8,64]{4,3,2,1,0:T(8,128)}) fusion(bf16[32,2,64,3,64]{4,3,2,1,0:T(4,128)(2,1)} %copy.21, s32[32,2,3]{2,1,0:T(2,128)S(1)} %copy.19), kind=kOutput, calls=%fused_computation.70 | convolution fusion | flops 14681600 | bytes 14156544 | tf_op jit(solution)/shard_map/tikc,tiakb->tiacb/dot_general | solution.py:55
  29.0 11.9 %convert_element_type.77 = bf16[32,2,64,512]{3,2,1,0:T(8,128)(2,1)} reshape(bf16[32,2,64,8,64]{4,3,2,1,0:T(8,128)(2,1)} %get-tuple-element.196) | data formatting | bytes 8388608 | tf_op jit(solution)/shard_map/convert_element_type | solution.py:57
  41.4 8.7 %fusion.28 = bf16[32,2,64,512]{3,1,2,0:T(2,128)(2,1)S(1)} fusion(bf16[32,2,64,512]{3,2,1,0:T(8,128)(2,1)} %convert_element_type.77, s32[2]{0:T(128)S(1)} %iota_add_fusion, s32[32,2]{1,0:T(8,128)S(1)} %copy.22), kind=kOutput, calls=%fused_computation.42 | convolution fusion | flops 8388736 | bytes 8388872 | tf_op jit(solution)/shard_map/tos,tsbn->tobn/dot_general | solution.py:60
  53.4 6.4 copy.24
  60.0 14.5 %reshape_reshape.3 = f32[32,128,512]{2,1,0:T(8,128)} reshape(f32[32,2,64,8,64]{4,3,2,1,0:T(8,128)} %get-tuple-element.197) | data formatting | bytes 16777216 | tf_op jit(solution)/shard_map/reshape;reshape | solution.py:92
  74.4 9.0 %copy.25 = f32[32,128,512]{1,2,0:T(8,128)} copy(f32[32,128,512]{2,1,0:T(8,128)} %reshape_reshape.3) | data formatting | bytes 16777216 | tf_op jit(solution)/shard_map/reshape;reshape | solution.py:92
  83.5 63.2 %all-reduce.2.cloned.1.call-done = bf16[32,128,512]{1,2,0:T(8,128)(2,1)} async-done(((bf16[32,128,512]{1,2,0:T(8,128)(2,1)}), bf16[32,128,512]{1,2,0:T(8,128)(2,1)}) %all-reduce.2.cloned.1.call-update) | async-done | bytes 4194320 | tf_op jit(solution)/shard_map/psum | solution.py:82
  146.7 7.9 %fusion.23 = bf16[32,128,512]{1,2,0:T(8,128)(2,1)} fusion(f32[32,128,512]{1,2,0:T(8,128)} %copy.25, bf16[32,128,128]{2,1,0:T(8,128)(2,1)S(1)} %copy-done, bf16[32,128,512]{1,2,0:T(8,128)(2,1)} %all-reduce.2.cloned.1.call-done, pred[32,128]{1,0:T(8,128)(4,1)S(1)} %iota_compare_fusion.2), kind=kOutput, calls=%fused_computation.36 | convolution fusion | flops 543162368 | bytes 17829888 | tf_op jit(solution)/shard_map/tro,ton->trn/dot_general | solution.py:91
  156.4 90.4 %collective-permute-done.1 = bf16[32,128,512]{1,2,0:T(8,128)(2,1)} collective-permute-done((bf16[32,128,512]{1,2,0:T(8,128)(2,1)}, bf16[32,128,512]{1,2,0:T(8,128)(2,1)}, u32[]{:S(2)}, u32[]{:S(2)}) %collective-permute-start.1) | collective-permute-done | bytes 4194336 | tf_op jit(solution)/shard_map/ppermute | solution.py:21
  248.2 47.8 %psum.15 = bf16[32,128]{1,0:T(8,128)(2,1)S(1)} all-reduce(bf16[32,128]{1,0:T(8,128)(2,1)S(1)} %convert_element_type.84), channel_id=1, replica_groups=mesh['tm'=8,'state'=4] {'state'}, use_global_device_ids=true, to_apply=%region_1.0 | all-reduce | flops 4096 | bytes 16384 | tf_op jit(solution)/shard_map/psum | solution.py:83
  297.8 5.4 all_gather.6
  303.3 6.5 copy.26
  309.8 6.7 broadcast_in_dim.39
  318.9 6.5 copy.27
  325.4 6.5 copy.28
  331.9 4.7 constant_dynamic-update-slice_fusion.2
  339.0 6.5 copy.29
  345.5 4.5 constant_dynamic-update-slice_fusion
  350.0 173.2 %while.42 = (s32[]{:T(128)}, f32[512,128]{1,0:T(8,128)S(1)}, f32[512]{0:T(512)S(1)}, bf16[32,512,512]{2,1,0:T(8,128)(2,1)}, f32[32,512]{1,0:T(8,128)S(1)}) while((s32[]{:T(128)}, f32[512,128]{1,0:T(8,128)S(1)}, f32[512]{0:T(512)S(1)}, bf16[32,512,512]{2,1,0:T(8,128)(2,1)}, f32[32,512]{1,0:T(8,128)S(1)}) %tuple.65), condition=%wide.region_3.4_spmd.clone.clone, body=%wide.region_2.3_spmd.clone.sunk.clone | while | flops 135597568 | bytes 4357196 | solution.py:109
  524.1 16.9 %all-gather.2.cloned.1.call-done = f32[512,512]{1,0:T(8,128)} async-done(((f32[512,128]{1,0:T(8,128)}), f32[512,512]{1,0:T(8,128)}) %all-gather.2.cloned.1.call-update) | async-done | bytes 1048592 | tf_op jit(solution)/shard_map/all_gather | solution.py:112
  541.0 60.1 %while.40 = (s32[]{:T(128)}, f32[512]{0:T(512)S(1)}, pred[]{:T(512)}, f32[512,512]{1,0:T(8,128)}, f32[512]{0:T(512)S(1)}, /*index=5*/f32[512]{0:T(512)S(1)}) while((s32[]{:T(128)}, f32[512]{0:T(512)S(1)}, pred[]{:T(512)}, f32[512,512]{1,0:T(8,128)}, f32[512]{0:T(512)S(1)}, /*index=5*/f32[512]{0:T(512)S(1)}) %tuple.79), condition=%wide.region_5.6_spmd.clone, body=%wide.region_4.5_spmd.sunk.clone | while | flops 3146754 | bytes 1073262 | solution.py:120
  601.1 127.8 %while.41 = (s32[]{:T(128)}, f32[512]{0:T(512)S(1)}, f32[32,128]{1,0:T(8,128)}, bf16[32,512,512]{2,1,0:T(8,128)(2,1)}, f32[32,512]{1,0:T(8,128)S(1)}, /*index=5*/s32[]{:T(128)}) while((s32[]{:T(128)}, f32[512]{0:T(512)S(1)}, f32[32,128]{1,0:T(8,128)}, bf16[32,512,512]{2,1,0:T(8,128)(2,1)}, f32[32,512]{1,0:T(8,128)S(1)}, ...), condition=%wide.region_7.8_spmd.clone, body=%wide.region_6.7_spmd.sunk.clone | while | flops 1051650 | bytes 1081425 | solution.py:127
  (791 shorter events, 372.9 us)
Async XLA Ops:
  6.5 140.2 %copy-start = (bf16[32,128,128]{2,1,0:T(8,128)(2,1)S(1)}, bf16[32,128,128]{2,1,0:T(8,128)(2,1)}, u32[]{:S(2)}) copy-start(bf16[32,128,128]{2,1,0:T(8,128)(2,1)} %param.21) | copy-start | bytes 3145732
  6.5 140.2 %all-reduce.2.cloned.1.call-start = ((), (), s32[]{:S(2)}) async-start(), calls=%async_computation | async-start | bytes 8388608 | tf_op jit(solution)/shard_map/psum | solution.py:82
  11.1 7.2 copy-start.8
  29.0 11.9 %copy-start.10 = (s32[32,2]{0,1:T(2,128)S(1)}, s32[32,2]{0,1:T(2,128)}, u32[]{:S(2)}) copy-start(s32[32,2]{0,1:T(2,128)} %param.17) | copy-start | bytes 772
  29.0 12.0 %copy-start.4 = (bf16[32,64,128]{2,1,0:T(8,128)(2,1)S(1)}, bf16[32,64,128]{2,1,0:T(8,128)(2,1)}, u32[]{:S(2)}) copy-start(bf16[32,64,128]{2,1,0:T(8,128)(2,1)} %param.18) | copy-start | bytes 1572868
  59.9 481.1 %all-gather.2.cloned.1.call-start = ((), (), s32[]{:S(2)}) async-start(), calls=%async_computation.1 | async-start | bytes 1310720 | tf_op jit(solution)/shard_map/all_gather | solution.py:112
  74.4 9.0 %copy-start.9 = (s32[32]{0:T(128)S(1)}, s32[32]{0:T(128)}, u32[]{:S(2)}) copy-start(s32[32]{0:T(128)} %param.19) | copy-start | bytes 388
  83.5 163.3 %copy-start.6 = (f32[32,128]{1,0:T(8,128)S(1)}, f32[32,128]{1,0:T(8,128)}, u32[]{:S(2)}) copy-start(f32[32,128]{1,0:T(8,128)} %param.22) | copy-start | bytes 49156
  83.5 212.5 %copy-start.7 = (f32[32,128]{1,0:T(8,128)S(1)}, f32[32,128]{1,0:T(8,128)}, u32[]{:S(2)}) copy-start(f32[32,128]{1,0:T(8,128)} %param.20) | copy-start | bytes 49156
  154.6 92.2 %collective-permute-start.1 = (bf16[32,128,512]{1,2,0:T(8,128)(2,1)}, bf16[32,128,512]{1,2,0:T(8,128)(2,1)}, u32[]{:S(2)}, u32[]{:S(2)}) collective-permute-start(bf16[32,128,512]{1,2,0:T(8,128)(2,1)} %fusion.23), channel_id=1, source_target_pairs={{0,1},{1,2},{2,3},{3,0},{4,5},{5,6},{6,7},{7,4},{8,9},{9,10},{10,1... | collective-permute-start | bytes 12582920 | tf_op jit(solution)/shard_map/ppermute | solution.py:21
  154.6 170.8 %collective-permute-start.2 = (bf16[32,128,512]{1,2,0:T(8,128)(2,1)}, bf16[32,128,512]{1,2,0:T(8,128)(2,1)}, u32[]{:S(2)}, u32[]{:S(2)}) collective-permute-start(bf16[32,128,512]{1,2,0:T(8,128)(2,1)} %fusion.23), channel_id=1, source_target_pairs={{0,3},{1,0},{2,1},{3,2},{4,7},{5,4},{6,5},{7,6},{8,11},{9,8},{10,9... | collective-permute-start | bytes 12582920 | tf_op jit(solution)/shard_map/ppermute | solution.py:24
  246.8 92.2 %collective-permute-start.3 = (bf16[32,128,512]{1,2,0:T(8,128)(2,1)}, bf16[32,128,512]{1,2,0:T(8,128)(2,1)}, u32[]{:S(2)}, u32[]{:S(2)}) collective-permute-start(bf16[32,128,512]{1,2,0:T(8,128)(2,1)} %collective-permute-done.1), channel_id=1, source_target_pairs={{0,1},{1,2},{2,3},{3,0},{4,5},{5,6},{6,7},{7,4},{8,9},{9,10},{10,1... | collective-permute-start | bytes 12582920 | tf_op jit(solution)/shard_map/ppermute | solution.py:21
  309.8 6.7 copy-start.2
  331.9 4.7 copy-start.1
  350.0 174.0 %copy-start.5 = (f32[512]{0:T(512)S(1)}, f32[512]{0:T(512)}, u32[]{:S(2)}) copy-start(f32[512]{0:T(512)} %param.23) | copy-start | bytes 6148
  523.3 0.7 copy-start.3
  543.2 6.4 collective-permute-start
  551.8 6.4 collective-permute-start
  560.4 6.4 collective-permute-start
  569.0 6.4 collective-permute-start
  577.6 6.4 collective-permute-start
  586.2 6.4 collective-permute-start
  594.8 6.4 collective-permute-start
Sparse Core Ops, SparseCore 0:
  60.0 86.6 all-reduce.1
  524.2 16.8 all-gather.1
